TPU v7x, 256 devices: a whole 4x4x8 slice. The times are simulated.
256 devices in a mesh: lat: 8 (over y, z_hi), lon: 32 (over x, z_lo, core).
Axes of the slice: x: 4, y: 4, z: 8 (z_hi: 2, z_lo: 4; z = z_hi * 4 + z_lo), core: 2. Of those that a mesh axis runs over, the one named last changes fastest.
Arguments:
- sea_level: float32 [4096, 1024], P('lon', 'lat'), may hold values from -1 to 5
- east_velocity: float32 [4096, 1024], P('lon', 'lat'), may hold values from -6 to 6
- north_velocity: float32 [4096, 1024], P('lon', 'lat'), may hold values from -6 to 6
- depth: float32 [4096, 1024], P('lon', 'lat'), may hold values from 0.25 to 1
- land_mask: int32 [4096, 1024], P('lon', 'lat'), may hold values from 0 to 1, as said below
- wet_counts: int32 [8, 32], replicated, may hold values from 1 to 16384, as said below
- loading_prev: float32 [4096, 1024], P('lon', 'lat'), may hold values from -4 to 4
- tide_amp: float32 [8], replicated, may hold values from 0.3 to 1
- tide_phase: float32 [8], replicated, may hold values from -3.140625 to 3.140625
- legendre: bfloat16 [1024, 1024, 1024], P('lon', None, 'lat'), may hold values from -0.1875 to 0.1875
- love_factor: float32 [1024], replicated, may hold values from 0.05 to 1
Outputs:
- height_new: float32 [4096, 1024], P('lon', 'lat')
- east_new: float32 [4096, 1024], P('lon', 'lat')
- north_new: float32 [4096, 1024], P('lon', 'lat')
- self_attraction: float32 [4096, 1024], P('lon', 'lat')
Inputs may be any that keep to these rules, and one draw needn't show every extreme that they name: `land_mask`: every tile of 128 columns by 128 rows holds at least one wet column, and one tile is wholly wet. wet_counts[p, q] is the number of wet columns of land_mask in latitude band p and longitude band q.
All inputs are finite; a program needn't handle non-finite values.
Results may differ from a plain program's by a relative error of at most 0.0038.
Values may be sent and summed in bfloat16 or wider, within the bound.
A program may use at most 64 MiB of HBM per device.

v0:
```python
import math
import jax
import jax.numpy as jnp
from jax import lax
from jax.sharding import Mesh
from jax.sharding import PartitionSpec as P

SUBSTEPS = 4
LON = ("lon_0", "lon_1", "lon_2")
LAT = ("lat_0", "lat_1")
LAT_LON = ("lat_0", "lat_1", "lon_0", "lon_1", "lon_2")
lat_edge = 1.3089969
courant = 0.4
friction = 0.02
rotation = 0.2
frequencies = (0.1405, 0.1454, 0.1379, 0.1458, 0.0729, 0.0676, 0.0725, 0.0649)
orders = (2, 2, 2, 2, 1, 1, 1, 1)
highest = lax.Precision.HIGHEST


def padded(cells, sides, width, closed):
    for axis, dim in sides:
        count = lax.axis_size(axis)
        ends = count if closed else count - 1
        head = lax.slice_in_dim(cells, 0, width, axis=dim)
        tail = lax.slice_in_dim(cells, cells.shape[dim] - width, cells.shape[dim], axis=dim)
        cells = jnp.concatenate(
            [
                lax.ppermute(tail, axis, [(i, (i + 1) % count) for i in range(ends)]),
                cells,
                lax.ppermute(head, axis, [((i + 1) % count, i) for i in range(ends)]),
            ],
            axis=dim,
        )
    return cells


def one_axis_at_a_time(value, axes):
    for axis in axes:
        value = lax.psum(value, axis)
    return value


def in_blocks(value, dim, size):
    before, after = (value.shape[:dim], value.shape[dim + 1 :])
    return jnp.moveaxis(value.reshape(*before, size, -1, *after), dim, 0)


def sum_at_owner(value, axis, dim):
    size = lax.axis_size(axis)
    tiles = lax.all_to_all(in_blocks(value, dim, size), axis, 0, 0, tiled=True)
    return jnp.sum(tiles, axis=0)


def from_everyone(value, axis):
    copies = jnp.broadcast_to(value, (lax.axis_size(axis), *value.shape))
    return lax.all_to_all(copies, axis, split_axis=0, concat_axis=0, tiled=True)


def of_everyone(value, axis):
    return from_everyone(value, axis).sum(axis=0)


def latitude_of(rows, total_rows):
    return -lat_edge + 2.0 * lat_edge * (rows.astype(jnp.float32) + 0.5) / total_rows


def potential(columns, rows, moment, total_cols, total_rows, tide_amp, tide_phase):
    longitude = (2.0 * math.pi * (columns % total_cols).astype(jnp.float32) / total_cols)[:, None]
    latitude = latitude_of(rows, total_rows)[None, :]
    semi = jnp.cos(latitude) ** 2
    diurnal = jnp.sin(2.0 * latitude)
    field = jnp.zeros((columns.shape[0], rows.shape[0]), jnp.float32)
    for index in range(len(frequencies)):
        shape_term = semi if orders[index] == 2 else diurnal
        field = field + tide_amp[index] * shape_term * jnp.cos(
            frequencies[index] * moment + orders[index] * longitude + tide_phase[index]
        )
    return field * (total_cols / 64.0)


def advance(state_x, static_x, forcing, latitude_x):
    height_x, east_x, north_x = (state_x[0], state_x[1], state_x[2])
    depth_x, wet_x, loading_x = (static_x[0], static_x[1], static_x[2])
    cosine = jnp.cos(latitude_x)[None, :]
    secant_cycle = (1.0 / jnp.cos(latitude_x[1:-1]))[None, :]
    secant_core = (1.0 / jnp.cos(latitude_x[2:-2]))[None, :]
    coriolis = (rotation * jnp.sin(latitude_x[2:-2]))[None, :]
    flux_east = depth_x * east_x
    flux_north = depth_x * north_x * cosine
    divergence = (
        (
            flux_east[2:, 1:-1]
            - flux_east[:-2, 1:-1]
            + (flux_north[1:-1, 2:] - flux_north[1:-1, :-2])
        )
        * 0.5
        * secant_cycle
    )
    height_cycle = height_x[1:-1, 1:-1] - courant * divergence * wet_x[1:-1, 1:-1]
    pressure = height_cycle - forcing - loading_x[1:-1, 1:-1]
    slope_east = (pressure[2:, 1:-1] - pressure[:-2, 1:-1]) * 0.5 * secant_core
    slope_north = (pressure[1:-1, 2:] - pressure[1:-1, :-2]) * 0.5
    east = east_x[2:-2, 2:-2]
    north = north_x[2:-2, 2:-2]
    wet = wet_x[2:-2, 2:-2]
    east_next = wet * ((1.0 - friction) * east + courant * (coriolis * north - slope_east))
    north_next = wet * ((1.0 - friction) * north - courant * (coriolis * east + slope_north))
    return jnp.stack([height_cycle[1:-1, 1:-1], east_next, north_next])


def extend_margin(fields, margin):
    wide = padded(fields, ((LON, 1),), margin, True)
    return padded(wide, ((LAT, 2),), margin, False)


def wave_table(waves, columns, total_cols, weights):
    turns = waves[None, :] * columns[:, None] % total_cols
    angle = 2.0 * math.pi * turns.astype(jnp.float32) / total_cols
    scale = weights[None, :] / math.sqrt(total_cols)
    return jnp.stack([scale * jnp.cos(angle), -scale * jnp.sin(angle)], axis=2)


def shards(
    sea_level,
    east_velocity,
    north_velocity,
    depth,
    land_mask,
    wet_counts,
    loading_prev,
    tide_amp,
    tide_phase,
    legendre,
    love_factor,
):
    lon_dev, lat_dev = sea_level.shape
    wave_dev = legendre.shape[0]
    lon_count = lax.axis_size(LON)
    total_cols = lon_dev * lon_count
    total_rows = lat_dev * lax.axis_size(LAT)
    lon_index = lax.axis_index(LON)
    lon_start = lon_index * lon_dev
    lat_start = lax.axis_index(LAT) * lat_dev
    wet = land_mask.astype(jnp.float32)
    margin = 2 * SUBSTEPS
    full = extend_margin(
        jnp.stack([sea_level, east_velocity, north_velocity, depth, wet, loading_prev]), margin
    )
    state_x = full[:3]
    static_full = full[3:]
    wide_cols = full.shape[1]
    wide_rows = full.shape[2]
    for moment in range(SUBSTEPS):
        reach = margin - 2 * moment
        offset = margin - reach
        static_x = static_full[:, offset : wide_cols - offset, offset : wide_rows - offset]
        latitude_x = jnp.clip(
            latitude_of(
                lat_start + jnp.arange(-reach, lat_dev + reach, dtype=jnp.int32), total_rows
            ),
            -1.5,
            1.5,
        )
        columns = lon_start + jnp.arange(1 - reach, lon_dev + reach - 1, dtype=jnp.int32)
        rows = lat_start + jnp.arange(1 - reach, lat_dev + reach - 1, dtype=jnp.int32)
        forcing = potential(
            columns, rows, float(moment), total_cols, total_rows, tide_amp, tide_phase
        )
        state_x = advance(state_x, static_x, forcing, latitude_x)
    height = state_x[0]
    wet_sum = one_axis_at_a_time(jnp.sum(wet * height), LAT_LON)
    mean_level = wet_sum / jnp.sum(wet_counts.astype(jnp.float32))
    anomaly = wet * (height - mean_level)
    local_cols = lon_start + jnp.arange(lon_dev, dtype=jnp.int32)
    count = wave_dev * lax.axis_size(LON)
    waves = jnp.arange(count, dtype=jnp.int32)
    table = wave_table(waves, local_cols, total_cols, jnp.ones((count,), jnp.float32))
    table = jnp.transpose(table, (1, 2, 0)).reshape(2 * count, lon_dev)
    fourier = sum_at_owner(
        jnp.dot(table, anomaly, precision=highest, preferred_element_type=jnp.float32).reshape(
            count, 2, lat_dev
        ),
        LON,
        0,
    ).astype(jnp.bfloat16)
    coefficients = lax.dot_general(
        fourier, legendre, (((2,), (2,)), ((0,), (0,))), preferred_element_type=jnp.float32
    )
    coefficients = of_everyone(coefficients, LAT)
    scaled = (coefficients * love_factor[None, None, :]).astype(jnp.bfloat16)
    synthesis = lax.dot_general(
        scaled, legendre, (((2,), (1,)), ((0,), (0,))), preferred_element_type=jnp.float32
    )
    own_waves = lon_index * wave_dev + jnp.arange(wave_dev, dtype=jnp.int32)
    weights = jnp.where(own_waves == 0, 1.0, 2.0).astype(jnp.float32)
    flat_spectra = synthesis.reshape(2 * wave_dev, lat_dev)
    count = lon_dev * lax.axis_size(LON)
    cells = jnp.arange(count, dtype=jnp.int32)
    table = wave_table(own_waves, cells, total_cols, weights).reshape(count, 2 * wave_dev)
    self_attraction = sum_at_owner(
        jnp.dot(table, flat_spectra, precision=highest, preferred_element_type=jnp.float32), LON, 0
    )
    return (state_x[0], state_x[1], state_x[2], self_attraction)


def solution(mesh):
    torus = Mesh(mesh.devices.reshape(4, 2, 4, 4, 2), ("lat_0", "lat_1", "lon_0", "lon_1", "lon_2"))
    return jax.shard_map(
        shards,
        mesh=torus,
        in_specs=(
            P(LON, LAT),
            P(LON, LAT),
            P(LON, LAT),
            P(LON, LAT),
            P(LON, LAT),
            P(),
            P(LON, LAT),
            P(),
            P(),
            P(LON, None, LAT),
            P(),
        ),
        out_specs=(P(LON, LAT), P(LON, LAT), P(LON, LAT), P(LON, LAT)),
        check_vma=False,
    )
```

profile of v0, /device:TPU:1, one launch (start us, length us, event | category | flops | bytes accessed | tf_op | source)
XLA Modules:
  0.0 320.3 jit_solution(9844729480353911763)
XLA Ops:
  5.7 3.3 %collective-permute-start.1 = (f32[6,8,128]{2,1,0:T(8,128)S(1)}, f32[6,8,128]{2,1,0:T(8,128)S(1)}, u32[]{:S(2)}, u32[]{:S(2)}) collective-permute-start(f32[6,8,128]{2,1,0:T(8,128)S(1)} %get-tuple-element.50), channel_id=1, source_target_pairs={{1,0},{2,1},{3,2},{4,3},{5,4},{6,5},{7,6},{8,7},{9,8},{10,9},{11,1... | collective-permute-start | bytes 73736 | tf_op jit(solution)/shard_map/ppermute | solution.py:31
  9.1 1.6 fusion.112
  13.2 1.6 fusion.111
  17.5 1.4 add_cosine_fusion.2
  22.7 1.4 add_cosine_fusion.4
  24.1 1.4 add_cosine_fusion.12
  36.0 1.4 add_cosine_fusion.18
  38.6 1.4 add_cosine_fusion.20
  49.3 1.4 add_cosine_fusion.28
  55.2 1.4 collective-permute-start.3
  56.6 8.8 %collective-permute-start.2 = (f32[6,144,8]{2,1,0:T(8,128)S(1)}, f32[6,144,8]{2,1,0:T(8,128)S(1)}, u32[]{:S(2)}, u32[]{:S(2)}) collective-permute-start(f32[6,144,8]{2,1,0:T(8,128)S(1)} %get-tuple-element.47), channel_id=1, source_target_pairs={{0,32},{32,64},{64,96},{96,128},{128,160},{160,192},{192,224},{1,3... | collective-permute-start | bytes 82952 | tf_op jit(solution)/shard_map/ppermute | solution.py:29
  65.4 4.6 %collective-permute-done.3 = f32[6,144,8]{2,1,0:T(8,128)S(1)} collective-permute-done((f32[6,144,8]{2,1,0:T(8,128)S(1)}, f32[6,144,8]{2,1,0:T(8,128)S(1)}, u32[]{:S(2)}, u32[]{:S(2)}) %collective-permute-start.3) | collective-permute-done | bytes 27680 | tf_op jit(solution)/shard_map/ppermute | solution.py:31
  70.0 1.4 collective-permute-done.2
  76.6 27.8 %psum.35 = f32[]{:T(128)} all-reduce(f32[]{:T(128)} %get-tuple-element.4), channel_id=1, replica_groups=mesh['lat_0'=4,'lat_1'=2,'lon_0'=4,'lon_1'=4,'lon_2'=2] {'lat_0'}, use_global_device_ids=true, to_apply=%region_1.2 | all-reduce | flops 1 | bytes 8 | tf_op jit(solution)/shard_map/psum | solution.py:40
  104.4 2.1 cosine_multiply_fusion
  106.6 8.6 %psum.36 = f32[]{:T(128)} all-reduce(f32[]{:T(128)} %psum.35), channel_id=1, replica_groups=mesh['lat_0'=4,'lat_1'=2,'lon_0'=4,'lon_1'=4,'lon_2'=2] {'lat_1'}, use_global_device_ids=true, to_apply=%region_2.3 | all-reduce | flops 1 | bytes 8 | tf_op jit(solution)/shard_map/psum | solution.py:40
  115.3 11.1 %psum.37 = f32[]{:T(128)} all-reduce(f32[]{:T(128)} %psum.36), channel_id=1, replica_groups=mesh['lat_0'=4,'lat_1'=2,'lon_0'=4,'lon_1'=4,'lon_2'=2] {'lon_0'}, use_global_device_ids=true, to_apply=%region_3.4 | all-reduce | flops 1 | bytes 8 | tf_op jit(solution)/shard_map/psum | solution.py:40
  127.0 18.4 %psum.38 = f32[]{:T(128)} all-reduce(f32[]{:T(128)} %psum.37), channel_id=1, replica_groups=mesh['lat_0'=4,'lat_1'=2,'lon_0'=4,'lon_1'=4,'lon_2'=2] {'lon_1'}, use_global_device_ids=true, to_apply=%region_4.5 | all-reduce | flops 1 | bytes 8 | tf_op jit(solution)/shard_map/psum | solution.py:40
  145.7 10.4 %psum.39 = f32[]{:T(128)} all-reduce(f32[]{:T(128)} %psum.38), channel_id=1, replica_groups=mesh['lat_0'=4,'lat_1'=2,'lon_0'=4,'lon_1'=4,'lon_2'=2] {'lon_2'}, use_global_device_ids=true, to_apply=%region_5.6 | all-reduce | flops 1 | bytes 8 | tf_op jit(solution)/shard_map/psum | solution.py:40
  158.4 31.0 %all_to_all.15 = f32[32,32,2,128]{3,1,2,0:T(8,128)S(1)} all-to-all(f32[32,32,2,128]{3,1,2,0:T(8,128)S(1)} %fusion.2), channel_id=1, replica_groups=mesh['lat_0'=4,'lat_1'=2,'lon_0'=4,'lon_1'=4,'lon_2'=2] {'lon_0','lon_1'..., dimensions={0} | all-to-all | bytes 2097152 | tf_op jit(solution)/shard_map/all_to_all | solution.py:51
  189.5 5.6 %fusion.83 = f32[32,2,1024]{2,1,0:T(2,128)S(1)} fusion(bf16[32,1024,128]{2,1,0:T(8,128)(2,1)} %param.20, bf16[32,2,128]{2,0,1:T(8,128)(2,1)S(1)} %reduce_sum.47), kind=kOutput, calls=%fused_computation.148 | convolution fusion | flops 16777216 | bytes 8667136 | tf_op jit(solution)/shard_map/dot_general | solution.py:187
  195.2 1.6 broadcast_in_dim.10
  196.8 7.1 %all-to-all-start.1 = ((f32[8,32,2,1024]{3,1,2,0:T(8,128)}), f32[8,32,2,1024]{3,1,2,0:T(8,128)S(1)}, u32[]{:S(2)}, u32[]{:S(2)}) async-start(f32[8,32,2,1024]{3,1,2,0:T(8,128)} %broadcast_in_dim.10), calls=%async_computation.1 | async-start | bytes 4194304 | tf_op jit(solution)/shard_map/all_to_all | solution.py:57
  204.0 2.1 cosine_multiply_fusion.1
  206.2 1.8 copy.30
  208.0 2.1 dot_general.16
  210.2 44.3 %all-to-all-done.1 = f32[8,32,2,1024]{3,1,2,0:T(8,128)S(1)} async-done(((f32[8,32,2,1024]{3,1,2,0:T(8,128)}), f32[8,32,2,1024]{3,1,2,0:T(8,128)S(1)}, u32[]{:S(2)}, u32[]{:S(2)}) %all-to-all-start.1) | async-done | bytes 2097184 | tf_op jit(solution)/shard_map/all_to_all | solution.py:57
  254.6 4.6 %fusion.64 = f32[32,2,128]{2,1,0:T(2,128)S(1)} fusion(bf16[32,1024,128]{2,1,0:T(8,128)(2,1)} %param.20, bf16[32,2,1024]{2,0,1:T(8,128)(2,1)S(1)} %multiply_convert_fusion), kind=kOutput, calls=%fused_computation.120 | convolution fusion | flops 16777216 | bytes 8552448 | tf_op jit(solution)/shard_map/dot_general | solution.py:192
  259.2 5.1 %fusion = f32[32,128,128]{2,1,0:T(8,128)} fusion(f32[64,128,1]{1,0,2:T(8,128)S(1)} %bitcast.95, f32[32,128,64]{1,0,2:T(8,128)S(1)} %dot_general.16), kind=kOutput, calls=%fused_computation.2 | convolution fusion | flops 402653184 | bytes 3178496 | tf_op jit(solution)/shard_map/dot_general | solution.py:202
  264.2 5.5 %all-to-all-start.2 = ((f32[32,128,128]{2,1,0:T(8,128)}), f32[32,128,128]{2,1,0:T(8,128)S(1)}, u32[]{:S(2)}, u32[]{:S(2)}) async-start(f32[32,128,128]{2,1,0:T(8,128)} %fusion), calls=%async_computation.2 | async-start | bytes 4194304 | tf_op jit(solution)/shard_map/all_to_all | solution.py:51
  269.9 1.9 fusion.72
  271.8 47.8 %all-to-all-done.2 = f32[32,128,128]{2,1,0:T(8,128)S(1)} async-done(((f32[32,128,128]{2,1,0:T(8,128)}), f32[32,128,128]{2,1,0:T(8,128)S(1)}, u32[]{:S(2)}, u32[]{:S(2)}) %all-to-all-start.2) | async-done | bytes 2097184 | tf_op jit(solution)/shard_map/all_to_all | solution.py:51
  (87 shorter events, 48.0 us)
Async XLA Ops:
  5.7 49.2 %collective-permute-start.1 = (f32[6,8,128]{2,1,0:T(8,128)S(1)}, f32[6,8,128]{2,1,0:T(8,128)S(1)}, u32[]{:S(2)}, u32[]{:S(2)}) collective-permute-start(f32[6,8,128]{2,1,0:T(8,128)S(1)} %get-tuple-element.50), channel_id=1, source_target_pairs={{1,0},{2,1},{3,2},{4,3},{5,4},{6,5},{7,6},{8,7},{9,8},{10,9},{11,1... | collective-permute-start | bytes 73736 | tf_op jit(solution)/shard_map/ppermute | solution.py:31
  9.0 45.9 %collective-permute-start = (f32[6,8,128]{2,1,0:T(8,128)S(1)}, f32[6,8,128]{2,1,0:T(8,128)S(1)}, u32[]{:S(2)}, u32[]{:S(2)}) collective-permute-start(f32[6,8,128]{2,1,0:T(8,128)S(1)} %get-tuple-element.49), channel_id=1, source_target_pairs={{0,1},{1,2},{2,3},{3,4},{4,5},{5,6},{6,7},{7,8},{8,9},{9,10},{10,1... | collective-permute-start | bytes 73736 | tf_op jit(solution)/shard_map/ppermute | solution.py:29
  55.2 20.7 %copy-start.1 = (s32[128,128]{1,0:T(8,128)S(1)}, s32[128,128]{1,0:T(8,128)}, u32[]{:S(2)}) copy-start(s32[128,128]{1,0:T(8,128)} %param.15) | copy-start | bytes 196612
  55.2 14.8 %collective-permute-start.3 = (f32[6,144,8]{2,1,0:T(8,128)S(1)}, f32[6,144,8]{2,1,0:T(8,128)S(1)}, u32[]{:S(2)}, u32[]{:S(2)}) collective-permute-start(f32[6,144,8]{2,1,0:T(8,128)S(1)} %get-tuple-element.48), channel_id=1, source_target_pairs={{32,0},{64,32},{96,64},{128,96},{160,128},{192,160},{224,192},{33,... | collective-permute-start | bytes 82952 | tf_op jit(solution)/shard_map/ppermute | solution.py:31
  56.6 14.8 %collective-permute-start.2 = (f32[6,144,8]{2,1,0:T(8,128)S(1)}, f32[6,144,8]{2,1,0:T(8,128)S(1)}, u32[]{:S(2)}, u32[]{:S(2)}) collective-permute-start(f32[6,144,8]{2,1,0:T(8,128)S(1)} %get-tuple-element.47), channel_id=1, source_target_pairs={{0,32},{32,64},{64,96},{96,128},{128,160},{160,192},{192,224},{1,3... | collective-permute-start | bytes 82952 | tf_op jit(solution)/shard_map/ppermute | solution.py:29
  71.9 4.0 %copy-start = (f32[132,132]{1,0:T(8,128)}, f32[132,132]{1,0:T(8,128)S(1)}, u32[]{:S(2)}) copy-start(f32[132,132]{1,0:T(8,128)S(1)} %get-tuple-element.43) | copy-start | bytes 209092
  72.1 54.3 %copy-start.4 = (s32[8,32]{1,0:T(8,128)S(1)}, s32[8,32]{1,0:T(8,128)}, u32[]{:S(2)}) copy-start(s32[8,32]{1,0:T(8,128)} %param.16) | copy-start | bytes 3076
  76.6 118.5 %copy-start.2 = (f32[128,128]{1,0:T(8,128)}, f32[128,128]{1,0:T(8,128)S(1)}, u32[]{:S(2)}) copy-start(f32[128,128]{1,0:T(8,128)S(1)} %get-tuple-element.5) | copy-start | bytes 196612
  195.1 59.4 %copy-start.3 = (f32[1024]{0:T(1024)S(1)}, f32[1024]{0:T(1024)}, u32[]{:S(2)}) copy-start(f32[1024]{0:T(1024)} %param.21) | copy-start | bytes 12292
  196.8 57.6 %all-to-all-start.1 = ((f32[8,32,2,1024]{3,1,2,0:T(8,128)}), f32[8,32,2,1024]{3,1,2,0:T(8,128)S(1)}, u32[]{:S(2)}, u32[]{:S(2)}) async-start(f32[8,32,2,1024]{3,1,2,0:T(8,128)} %broadcast_in_dim.10), calls=%async_computation.1 | async-start | bytes 4194304 | tf_op jit(solution)/shard_map/all_to_all | solution.py:57
  264.2 55.3 %all-to-all-start.2 = ((f32[32,128,128]{2,1,0:T(8,128)}), f32[32,128,128]{2,1,0:T(8,128)S(1)}, u32[]{:S(2)}, u32[]{:S(2)}) async-start(f32[32,128,128]{2,1,0:T(8,128)} %fusion), calls=%async_computation.2 | async-start | bytes 4194304 | tf_op jit(solution)/shard_map/all_to_all | solution.py:51
where the time goes:
time: 322 us; the launch traced here: 320 us
  blocking collectives  107 us (33%)
  waiting for transfers between devices  98 us (30%)
  other arithmetic  56.1 us (17%)
  starting transfers between devices  26.2 us (8%)
  matrix products  16.3 us (5%)
  local copies, waits for them, and re-layouts  14.1 us (4%)
    psum x5, blocking collectives, one_axis_at_a_time(): value = lax.psum(value, axis)  76.3 us
    all_to_all x1, waiting for transfers between devices, sum_at_owner(): tiles = lax.all_to_all(in_blocks(value, dim, size), axis, 0, 0, tiled=True)  47.8 us
    all_to_all x1, waiting for transfers between devices, from_everyone(): return lax.all_to_all(copies, axis, split_axis=0, concat_axis=0, tiled=True)  44.3 us
    all_to_all x1, blocking collectives, sum_at_owner(): tiles = lax.all_to_all(in_blocks(value, dim, size), axis, 0, 0, tiled=True)  31 us
    cos x16, other arithmetic, potential(): jnp.cos(frequencies[index] * moment + orders[index] * longitude + tide_ph...  21.2 us
    mul x16, other arithmetic, potential(): tide_amp[index] * shape_term  20.3 us
    ppermute x2, starting transfers between devices, padded(): lax.ppermute(tail, axis, [(i, (i + 1) % count) for i in range(ends)])  8.8 us
    all_to_all x1, starting transfers between devices, from_everyone(): return lax.all_to_all(copies, axis, split_axis=0, concat_axis=0, tiled=True)  7.15 us
  transfers between devices with their start and end apart: 6, of which 4 were waited for; matrix products, arithmetic and copies ran while one was open for 17% of the time, Pallas kernels for 0%

commit v1 on v0

--- a/solution.py
+++ b/solution.py
@@ -37,7 +37,8 @@
 
 def one_axis_at_a_time(value, axes):
     for axis in axes:
-        value = lax.psum(value, axis)
+        parts = lax.all_gather(value, axis, axis=0, tiled=False)
+        value = parts.sum(axis=0)
     return value
 
 

time: 322 us -> 341 us (1.059)
  other arithmetic: 56.1 us -> 70.5 us
  local copies, waits for them, and re-layouts: 14.1 us -> 25 us
    psum x5 -> x0, blocking collectives: 76.3 us -> none  [one_axis_at_a_time(): value = lax.psum(value, axis)]
    unnamed x0 -> x5, blocking collectives: none -> 72.9 us
    unnamed x14 -> x41, local copies, waits for them, and re-layouts: 3.4 us -> 14.3 us
  transfers between devices with their start and end apart: 6 -> 6, of which waited for: 4 -> 4; matrix products, arithmetic and copies ran while one was open for 17% -> 20% of each run, Pallas kernels for 0% -> 0%
where the time goes in v1:
time: 341 us; the launch traced here: 340 us
  blocking collectives  104 us (30%)
  waiting for transfers between devices  95.3 us (28%)
  other arithmetic  70.5 us (21%)
  starting transfers between devices  26.2 us (8%)
  local copies, waits for them, and re-layouts  25 us (7%)
  matrix products  16.2 us (5%)
    unnamed x5, blocking collectives  72.9 us
    all_to_all x1, waiting for transfers between devices, sum_at_owner(): tiles = lax.all_to_all(in_blocks(value, dim, size), axis, 0, 0, tiled=True)  47.8 us
    all_to_all x1, waiting for transfers between devices, from_everyone(): return lax.all_to_all(copies, axis, split_axis=0, concat_axis=0, tiled=True)  44.2 us
    all_to_all x1, blocking collectives, sum_at_owner(): tiles = lax.all_to_all(in_blocks(value, dim, size), axis, 0, 0, tiled=True)  31 us
    cos x16, other arithmetic, potential(): jnp.cos(frequencies[index] * moment + orders[index] * longitude + tide_ph...  23.6 us
    mul x16, other arithmetic, potential(): tide_amp[index] * shape_term  23.1 us
    unnamed x41, local copies, waits for them, and re-layouts  14.3 us
    ppermute x2, starting transfers between devices, padded(): lax.ppermute(tail, axis, [(i, (i + 1) % count) for i in range(ends)])  8.8 us
  transfers between devices with their start and end apart: 6, of which 4 were waited for; matrix products, arithmetic and copies ran while one was open for 20% of the time, Pallas kernels for 0%

profile of v1, /device:TPU:1, one launch (start us, length us, event | category | flops | bytes accessed | tf_op | source)
XLA Modules:
  0.0 339.5 jit_solution(10638622199405386326)
XLA Ops:
  5.7 3.3 collective-permute-start.1
  10.3 1.6 fusion.112
  13.2 1.9 add_cosine_fusion.8
  15.0 1.6 fusion.111
  17.9 1.9 broadcast_multiply_fusion.10
  21.2 1.9 add_cosine_fusion.10
  24.4 1.9 broadcast_multiply_fusion.12
  27.6 1.9 add_cosine_fusion.12
  30.8 1.9 broadcast_multiply_fusion.15
  34.1 1.9 add_cosine_fusion.14
  37.3 1.9 broadcast_multiply_fusion.17
  60.8 2.1 cosine_multiply_fusion
  67.4 8.8 %collective-permute-start.2 = (f32[6,144,8]{2,1,0:T(8,128)S(1)}, f32[6,144,8]{2,1,0:T(8,128)S(1)}, u32[]{:S(2)}, u32[]{:S(2)}) collective-permute-start(f32[6,144,8]{2,1,0:T(8,128)S(1)} %get-tuple-element.47), channel_id=1, source_target_pairs={{0,32},{32,64},{64,96},{96,128},{128,160},{160,192},{192,224},{1,3... | collective-permute-start | bytes 82952 | tf_op jit(solution)/shard_map/ppermute | solution.py:29
  78.9 1.9 collective-permute-done.3
  86.0 1.7 fusion.67
  91.5 27.2 %all-reduce = f32[4]{0:T(128)S(1)} all-reduce(f32[4]{0:T(128)S(1)} %dynamic-update-slice), channel_id=1, replica_groups=mesh['lat_0'=4,'lat_1'=2,'lon_0'=4,'lon_1'=4,'lon_2'=2] {'lat_0'}, use_global_device_ids=true, to_apply=%add | all-reduce | flops 4 | bytes 32
  121.3 7.9 %all-reduce.1 = f32[2]{0:T(128)S(1)} all-reduce(f32[2]{0:T(128)S(1)} %dynamic-update-slice.1), channel_id=1, replica_groups=mesh['lat_0'=4,'lat_1'=2,'lon_0'=4,'lon_1'=4,'lon_2'=2] {'lat_1'}, use_global_device_ids=true, to_apply=%add.1 | all-reduce | flops 2 | bytes 16
  131.8 10.6 %all-reduce.2 = f32[4]{0:T(128)S(1)} all-reduce(f32[4]{0:T(128)S(1)} %dynamic-update-slice.2), channel_id=1, replica_groups=mesh['lat_0'=4,'lat_1'=2,'lon_0'=4,'lon_1'=4,'lon_2'=2] {'lon_0'}, use_global_device_ids=true, to_apply=%add.2 | all-reduce | flops 4 | bytes 32
  145.0 17.6 %all-reduce.3 = f32[4]{0:T(128)S(1)} all-reduce(f32[4]{0:T(128)S(1)} %dynamic-update-slice.3), channel_id=1, replica_groups=mesh['lat_0'=4,'lat_1'=2,'lon_0'=4,'lon_1'=4,'lon_2'=2] {'lon_1'}, use_global_device_ids=true, to_apply=%add.3 | all-reduce | flops 4 | bytes 32
  165.2 9.5 %all-reduce.4 = f32[2]{0:T(128)S(1)} all-reduce(f32[2]{0:T(128)S(1)} %dynamic-update-slice.4), channel_id=1, replica_groups=mesh['lat_0'=4,'lat_1'=2,'lon_0'=4,'lon_1'=4,'lon_2'=2] {'lon_2'}, use_global_device_ids=true, to_apply=%add.4 | all-reduce | flops 2 | bytes 16
  177.7 31.0 %all_to_all.15 = f32[32,32,2,128]{3,1,2,0:T(8,128)S(1)} all-to-all(f32[32,32,2,128]{3,1,2,0:T(8,128)S(1)} %fusion.2), channel_id=1, replica_groups=mesh['lat_0'=4,'lat_1'=2,'lon_0'=4,'lon_1'=4,'lon_2'=2] {'lon_0','lon_1'..., dimensions={0} | all-to-all | bytes 2097152 | tf_op jit(solution)/shard_map/all_to_all | solution.py:52
  208.7 5.6 %fusion.83 = f32[32,2,1024]{2,1,0:T(2,128)S(1)} fusion(bf16[32,1024,128]{2,1,0:T(8,128)(2,1)} %param.20, bf16[32,2,128]{2,0,1:T(8,128)(2,1)S(1)} %reduce_sum.97), kind=kOutput, calls=%fused_computation.148 | convolution fusion | flops 16777216 | bytes 8667136 | tf_op jit(solution)/shard_map/dot_general | solution.py:188
  216.1 7.1 %all-to-all-start.1 = ((f32[8,32,2,1024]{3,1,2,0:T(8,128)}), f32[8,32,2,1024]{3,1,2,0:T(8,128)S(1)}, u32[]{:S(2)}, u32[]{:S(2)}) async-start(f32[8,32,2,1024]{3,1,2,0:T(8,128)} %broadcast_in_dim.10), calls=%async_computation.1 | async-start | bytes 4194304 | tf_op jit(solution)/shard_map/all_to_all | solution.py:58
  223.2 2.1 cosine_multiply_fusion.1
  225.5 1.8 copy.30
  227.3 2.1 dot_general.16
  229.4 44.2 %all-to-all-done.1 = f32[8,32,2,1024]{3,1,2,0:T(8,128)S(1)} async-done(((f32[8,32,2,1024]{3,1,2,0:T(8,128)}), f32[8,32,2,1024]{3,1,2,0:T(8,128)S(1)}, u32[]{:S(2)}, u32[]{:S(2)}) %all-to-all-start.1) | async-done | bytes 2097184 | tf_op jit(solution)/shard_map/all_to_all | solution.py:58
  273.8 4.6 %fusion.64 = f32[32,2,128]{2,1,0:T(2,128)S(1)} fusion(bf16[32,1024,128]{2,1,0:T(8,128)(2,1)} %param.20, bf16[32,2,1024]{2,0,1:T(8,128)(2,1)S(1)} %multiply_convert_fusion), kind=kOutput, calls=%fused_computation.120 | convolution fusion | flops 16777216 | bytes 8552448 | tf_op jit(solution)/shard_map/dot_general | solution.py:193
  278.4 5.1 %fusion = f32[32,128,128]{2,1,0:T(8,128)} fusion(f32[64,128,1]{1,0,2:T(8,128)S(1)} %bitcast.105, f32[32,128,64]{1,0,2:T(8,128)S(1)} %dot_general.16), kind=kOutput, calls=%fused_computation.2 | convolution fusion | flops 402653184 | bytes 3178496 | tf_op jit(solution)/shard_map/dot_general | solution.py:203
  283.4 5.6 %all-to-all-start.2 = ((f32[32,128,128]{2,1,0:T(8,128)}), f32[32,128,128]{2,1,0:T(8,128)S(1)}, u32[]{:S(2)}, u32[]{:S(2)}) async-start(f32[32,128,128]{2,1,0:T(8,128)} %fusion), calls=%async_computation.2 | async-start | bytes 4194304 | tf_op jit(solution)/shard_map/all_to_all | solution.py:52
  289.1 1.9 fusion.72
  291.0 47.8 %all-to-all-done.2 = f32[32,128,128]{2,1,0:T(8,128)S(1)} async-done(((f32[32,128,128]{2,1,0:T(8,128)}), f32[32,128,128]{2,1,0:T(8,128)S(1)}, u32[]{:S(2)}, u32[]{:S(2)}) %all-to-all-start.2) | async-done | bytes 2097184 | tf_op jit(solution)/shard_map/all_to_all | solution.py:52
  (119 shorter events, 69.0 us)
Async XLA Ops:
  5.7 60.0 %collective-permute-start.1 = (f32[6,8,128]{2,1,0:T(8,128)S(1)}, f32[6,8,128]{2,1,0:T(8,128)S(1)}, u32[]{:S(2)}, u32[]{:S(2)}) collective-permute-start(f32[6,8,128]{2,1,0:T(8,128)S(1)} %get-tuple-element.50), channel_id=1, source_target_pairs={{1,0},{2,1},{3,2},{4,3},{5,4},{6,5},{7,6},{8,7},{9,8},{10,9},{11,1... | collective-permute-start | bytes 73736 | tf_op jit(solution)/shard_map/ppermute | solution.py:31
  9.0 56.7 %collective-permute-start = (f32[6,8,128]{2,1,0:T(8,128)S(1)}, f32[6,8,128]{2,1,0:T(8,128)S(1)}, u32[]{:S(2)}, u32[]{:S(2)}) collective-permute-start(f32[6,8,128]{2,1,0:T(8,128)S(1)} %get-tuple-element.49), channel_id=1, source_target_pairs={{0,1},{1,2},{2,3},{3,4},{4,5},{5,6},{6,7},{7,8},{8,9},{9,10},{10,1... | collective-permute-start | bytes 73736 | tf_op jit(solution)/shard_map/ppermute | solution.py:29
  66.0 22.8 %copy-start.1 = (s32[128,128]{1,0:T(8,128)S(1)}, s32[128,128]{1,0:T(8,128)}, u32[]{:S(2)}) copy-start(s32[128,128]{1,0:T(8,128)} %param.15) | copy-start | bytes 196612
  66.0 14.8 %collective-permute-start.3 = (f32[6,144,8]{2,1,0:T(8,128)S(1)}, f32[6,144,8]{2,1,0:T(8,128)S(1)}, u32[]{:S(2)}, u32[]{:S(2)}) collective-permute-start(f32[6,144,8]{2,1,0:T(8,128)S(1)} %get-tuple-element.48), channel_id=1, source_target_pairs={{32,0},{64,32},{96,64},{128,96},{160,128},{192,160},{224,192},{33,... | collective-permute-start | bytes 82952 | tf_op jit(solution)/shard_map/ppermute | solution.py:31
  67.4 14.8 %collective-permute-start.2 = (f32[6,144,8]{2,1,0:T(8,128)S(1)}, f32[6,144,8]{2,1,0:T(8,128)S(1)}, u32[]{:S(2)}, u32[]{:S(2)}) collective-permute-start(f32[6,144,8]{2,1,0:T(8,128)S(1)} %get-tuple-element.47), channel_id=1, source_target_pairs={{0,32},{32,64},{64,96},{96,128},{128,160},{160,192},{192,224},{1,3... | collective-permute-start | bytes 82952 | tf_op jit(solution)/shard_map/ppermute | solution.py:29
  77.5 6.9 %copy-start.4 = (f32[136]{0:T(256)S(1)}, f32[136]{0:T(256)}, u32[]{:S(2)}) copy-start(f32[136]{0:T(256)} %get-tuple-element.55) | copy-start | bytes 1636
  77.5 6.9 %copy-start.5 = (f32[136]{0:T(256)S(1)}, f32[136]{0:T(256)}, u32[]{:S(2)}) copy-start(f32[136]{0:T(256)} %get-tuple-element.56) | copy-start | bytes 1636
  77.5 6.9 %copy-start.6 = (f32[136]{0:T(256)S(1)}, f32[136]{0:T(256)}, u32[]{:S(2)}) copy-start(f32[136]{0:T(256)} %get-tuple-element.114) | copy-start | bytes 1636
  80.8 10.1 %copy-start.10 = (u32[256]{0:T(256)S(1)}, u32[256]{0:T(256)}, u32[]{:S(2)}) copy-start(u32[256]{0:T(256)} %constant.358) | copy-start | bytes 3076
  80.8 39.9 %copy-start.9 = (u32[256]{0:T(256)S(1)}, u32[256]{0:T(256)}, u32[]{:S(2)}) copy-start(u32[256]{0:T(256)} %constant.363) | copy-start | bytes 3076
  80.8 50.4 %copy-start.8 = (u32[256]{0:T(256)S(1)}, u32[256]{0:T(256)}, u32[]{:S(2)}) copy-start(u32[256]{0:T(256)} %constant.368) | copy-start | bytes 3076
  80.8 63.6 %copy-start.7 = (u32[256]{0:T(256)S(1)}, u32[256]{0:T(256)}, u32[]{:S(2)}) copy-start(u32[256]{0:T(256)} %constant.373) | copy-start | bytes 3076
  82.7 80.5 %copy-start = (f32[132,132]{1,0:T(8,128)}, f32[132,132]{1,0:T(8,128)S(1)}, u32[]{:S(2)}) copy-start(f32[132,132]{1,0:T(8,128)S(1)} %get-tuple-element.43) | copy-start | bytes 209092
  89.5 126.6 %copy-start.2 = (f32[128,128]{1,0:T(8,128)}, f32[128,128]{1,0:T(8,128)S(1)}, u32[]{:S(2)}) copy-start(f32[128,128]{1,0:T(8,128)S(1)} %get-tuple-element.5) | copy-start | bytes 196612
  214.3 59.4 %copy-start.3 = (f32[1024]{0:T(1024)S(1)}, f32[1024]{0:T(1024)}, u32[]{:S(2)}) copy-start(f32[1024]{0:T(1024)} %param.21) | copy-start | bytes 12292
  216.1 57.6 %all-to-all-start.1 = ((f32[8,32,2,1024]{3,1,2,0:T(8,128)}), f32[8,32,2,1024]{3,1,2,0:T(8,128)S(1)}, u32[]{:S(2)}, u32[]{:S(2)}) async-start(f32[8,32,2,1024]{3,1,2,0:T(8,128)} %broadcast_in_dim.10), calls=%async_computation.1 | async-start | bytes 4194304 | tf_op jit(solution)/shard_map/all_to_all | solution.py:58
  283.4 55.3 %all-to-all-start.2 = ((f32[32,128,128]{2,1,0:T(8,128)}), f32[32,128,128]{2,1,0:T(8,128)S(1)}, u32[]{:S(2)}, u32[]{:S(2)}) async-start(f32[32,128,128]{2,1,0:T(8,128)} %fusion), calls=%async_computation.2 | async-start | bytes 4194304 | tf_op jit(solution)/shard_map/all_to_all | solution.py:52
